TPU v7x, 32 devices: a whole 2x2x4 slice. The times are simulated.
32 devices in a mesh: row: 4 (over x, core), col: 8 (over z, y).
Axes of the slice: x: 2, y: 2, z: 4, core: 2. Of those that a mesh axis runs over, the one named last changes fastest.
Arguments:
- orbitals: float32 [128, 32, 1024], P(('row', 'col')), may hold values from -6 to 6
- gradient: float32 [128, 32, 1024], P(('row', 'col')), may hold values from -4 to 4
- offsets: int32 [128, 3], replicated, may hold values from 0 to 3
- pairs: int32 [32, 4, 2], P('row'), may hold values from 0 to 127, as said below
- counts: int32 [32], P('row'), may hold values from 1 to 4, as said below
Outputs:
- updated: float32 [128, 32, 1024], P(('row', 'col'))
- energies: float32 [2], replicated
Inputs may be any that keep to these rules, and one draw needn't show every extreme that they name: `pairs`: both orbitals of a slot of pair owner p belong to p's group, ids g * 32 to (g + 1) * 32 - 1 with g = p // 8 (device d owns ids d * 4 onward). Among the live slots of one pair owner at most 2 distinct orbitals come from any one device, and every owner reaches 2 from some device. `counts`: every group of 8 pair owners has one owner with 4 live slots.
All inputs are finite; a program needn't handle non-finite values.
Results may differ from a plain program's by a relative error of at most 0.0082.
Values may be sent and summed in bfloat16 or wider, within the bound.
No kernel may reach another device: no remote copies, remote signals or barrier semaphores. Data moves between devices by JAX's collectives and lax.ppermute only.
A program may use at most 64 MiB of HBM per device.

v0:
```python
import jax
import jax.numpy as jnp
from jax import lax
from jax.sharding import PartitionSpec as P

CAP = 2
SHIFT = 4
SWEEPS = 12
ROUNDS = 2
screen_mu = 0.1
damping = 0.5


def sweep_table(sweeps):
    center_val = 6.0 + screen_mu
    half_width = 6.0
    ratio_val = center_val / half_width
    prev_coef = 1.0 / ratio_val
    keep_list = []
    mix_list = []
    for sweep_idx in range(sweeps):
        next_coef = 1.0 / (2.0 * ratio_val - prev_coef)
        keep_list.append(next_coef * prev_coef)
        mix_list.append(2.0 * next_coef / half_width)
        prev_coef = next_coef
    return (jnp.array(keep_list, jnp.float32), jnp.array(mix_list, jnp.float32), 1.0 / center_val)


def apply_operator(field):
    edge = field.shape[0]
    plane = field.shape[1]
    zero_row = jnp.zeros_like(field[:1])
    along_x = jnp.concatenate([field[1:], zero_row], 0) + jnp.concatenate([zero_row, field[:-1]], 0)
    zero_band = jnp.zeros_like(field[:, :edge])
    along_y = jnp.concatenate([field[:, edge:], zero_band], 1) + jnp.concatenate(
        [zero_band, field[:, :-edge]], 1
    )
    zero_col = jnp.zeros_like(field[:, :1])
    depth = jnp.arange(plane) % edge
    upper = jnp.where(depth < edge - 1, jnp.concatenate([field[:, 1:], zero_col], 1), 0.0)
    lower = jnp.where(depth > 0, jnp.concatenate([zero_col, field[:, :-1]], 1), 0.0)
    return (6.0 + screen_mu) * field - (along_x + along_y + upper + lower)


def screened_solve(source, tables):
    keep_coef, mix_coef, first_coef = tables

    def sweep(index, state):
        solution, remainder, direction = state
        solution = solution + direction
        remainder = remainder - apply_operator(direction)
        direction = keep_coef[index] * direction + mix_coef[index] * remainder
        return (solution, remainder, direction)

    state = (jnp.zeros_like(source), source, source * first_coef)
    return lax.fori_loop(0, keep_coef.shape[0], sweep, state)[0]


def displaced(box, shift):
    edge = box.shape[0]
    reach = SHIFT - 1
    cube = jnp.pad(box.reshape(edge, edge, edge), reach)
    start = shift + reach
    moved = lax.dynamic_slice(cube, (start[0], start[1], start[2]), (edge, edge, edge))
    return moved.reshape(edge, edge * edge)


def run_pairs(boxes, source_of, slot_of, mine, mine_count, group_offsets, tables, slots):
    edge = boxes.shape[1]
    plane = boxes.shape[2]
    collected = jnp.zeros((slots, edge, plane), jnp.float32)

    def one_pair(index, state):
        gathered, energy = state
        first = mine[index, 0]
        second = mine[index, 1]
        shift = group_offsets[first] - group_offsets[second]
        box_i = lax.dynamic_index_in_dim(boxes, source_of[first], 0, False).astype(jnp.float32)
        box_j = displaced(
            lax.dynamic_index_in_dim(boxes, source_of[second], 0, False), shift
        ).astype(jnp.float32)
        density = box_i * box_j
        potential = screened_solve(density, tables)
        term = potential * box_j
        target = slot_of[first]
        current = lax.dynamic_index_in_dim(gathered, target, 0, False)
        gathered = lax.dynamic_update_index_in_dim(gathered, current + term, target, 0)
        return (gathered, energy + jnp.sum(density * potential))

    return lax.fori_loop(0, mine_count, one_pair, (collected, jnp.zeros((), jnp.float32)))


def local(orbitals, gradient, offsets, pairs, counts):
    tables = sweep_table(SWEEPS)
    own_count = orbitals.shape[0]
    edge = orbitals.shape[1]
    plane = orbitals.shape[2]
    columns = lax.axis_size("col")
    own_index = lax.axis_index("col")
    group = columns * own_count
    slots = columns * CAP
    base = lax.axis_index("row") * group
    local_pairs = pairs - base
    group_offsets = lax.dynamic_slice_in_dim(offsets, base, group, 0)
    orbit_ids = jnp.arange(group, dtype=jnp.int32)
    live = jnp.arange(local_pairs.shape[1])[None, :] < counts[:, None]
    hits = (local_pairs[:, :, 0, None] == orbit_ids) | (local_pairs[:, :, 1, None] == orbit_ids)
    needed = (
        jnp.any(hits & live[:, :, None], axis=1)
        .astype(jnp.int32)
        .reshape(columns, columns, own_count)
    )
    ranks = jnp.cumsum(needed, axis=2) - 1
    send_need = lax.dynamic_index_in_dim(needed, own_index, 1, False)
    send_rank = lax.dynamic_index_in_dim(ranks, own_index, 1, False)
    slot_ids = jnp.arange(CAP)
    plan = (
        (send_need[:, None, :] == 1) & (send_rank[:, None, :] == slot_ids[None, :, None])
    ).astype(jnp.bfloat16)
    recv_rank = lax.dynamic_index_in_dim(ranks, own_index, 0, False)
    slot_of = (jnp.arange(columns)[:, None] * CAP + recv_rank).reshape(group)
    mine = lax.dynamic_index_in_dim(local_pairs, own_index, 0, False)
    mine_count = lax.dynamic_index_in_dim(counts, own_index, 0, False)
    current = orbitals
    totals = []
    for round_idx in range(ROUNDS):
        boxes_own = current.astype(jnp.bfloat16)
        outgoing = jnp.einsum(
            "pkm,mc->pkc",
            plan,
            boxes_own.reshape(own_count, edge * plane),
            preferred_element_type=jnp.float32,
        ).astype(jnp.bfloat16)
        arrived = lax.all_to_all(outgoing, "col", split_axis=0, concat_axis=0, tiled=True).reshape(
            slots, edge, plane
        )
        gathered, energy = run_pairs(
            arrived, slot_of, slot_of, mine, mine_count, group_offsets, tables, slots
        )
        slot_terms = gathered.astype(jnp.bfloat16).reshape(columns, CAP, edge * plane)
        returned = lax.all_to_all(slot_terms, "col", split_axis=0, concat_axis=0, tiled=True)
        exchange_term = jnp.einsum(
            "pkm,pkc->mc", plan, returned, preferred_element_type=jnp.float32
        )
        current = current - damping * (gradient + exchange_term.reshape(own_count, edge, plane))
        totals.append(energy)
    summed = lax.psum(jnp.stack(totals), ("row", "col"))
    energies = summed / (edge * edge * edge * lax.axis_size("row") * columns)
    return (current, energies)


def solution(mesh):
    return jax.shard_map(
        local,
        mesh=mesh,
        in_specs=(
            P(("row", "col"), None, None),
            P(("row", "col"), None, None),
            P(),
            P("row", None, None),
            P("row"),
        ),
        out_specs=(P(("row", "col"), None, None), P()),
        check_vma=False,
    )
```

profile of v0, /device:TPU:0, one launch (start us, length us, event | category | flops | bytes accessed | tf_op | source)
XLA Modules:
  0.0 598.3 jit_solution(14379024483895051703)
XLA Ops:
  4.1 2.1 copy.30
  6.1 7.3 %all-to-all-start = ((bf16[8,2,32768]{2,1,0:T(2,128)(2,1)}), bf16[8,2,32768]{2,1,0:T(2,128)(2,1)S(1)}, u32[]{:S(2)}, u32[]{:S(2)}) async-start(bf16[8,2,32768]{2,1,0:T(2,128)(2,1)} %copy.30), calls=%async_computation | async-start | bytes 2097152 | tf_op jit(solution)/shard_map/all_to_all | solution.py:134
  14.8 24.4 %all-to-all-done = bf16[8,2,32768]{2,1,0:T(2,128)(2,1)S(1)} async-done(((bf16[8,2,32768]{2,1,0:T(2,128)(2,1)}), bf16[8,2,32768]{2,1,0:T(2,128)(2,1)S(1)}, u32[]{:S(2)}, u32[]{:S(2)}) %all-to-all-start) | async-done | bytes 1048608 | tf_op jit(solution)/shard_map/all_to_all | solution.py:134
  39.2 1.6 reshape.110
  41.1 54.8 %while.91 = (s32[]{:T(128)}, f32[16,32,1024]{2,1,0:T(8,128)S(1)}, f32[]{:T(128)}, s32[]{:T(128)}, s32[4,2]{0,1:T(2,128)S(1)}, /*index=5*/s32[32]{0:T(128)S(1)}, ...) while((s32[]{:T(128)}, f32[16,32,1024]{2,1,0:T(8,128)S(1)}, ...), condition=%wide.region_6.7_spmd.clone, body=%wide.region_2.6_spmd.sunk.clone.sunk | while | flops 761891 | bytes 5591096 | solution.py:90
  59.2 34.8 %while.94 = (s32[]{:T(128)}, f32[32,1024]{1,0:T(8,128)S(1)}, f32[32,1024]{1,0:T(8,128)S(1)}, f32[32,1024]{1,0:T(8,128)S(1)}, s32[]{:T(128)}, /*index=5*/f32[12]{0:T(128)S(1)}, f32[12]{0:T(128)S(1)}, s32[]{:T(128)}) while((s32[]{:T(128)}, f32[32,1024]{1,0:T(8,128)S(1)}, f32[32,1024]{1,0:T(8,128)S(1)}, ...), condition=%wide.region_4.4_spmd.clone.clone, body=%wide.region_3.3_spmd.sunk.clone.clone.sunk | while | flops 499715 | bytes 3100039 | solution.py:56
  60.7 1.4 multiply_add_fusion.5
  63.6 1.4 multiply_add_fusion.5
  66.5 1.4 multiply_add_fusion.5
  69.4 1.4 multiply_add_fusion.5
  72.3 1.4 multiply_add_fusion.5
  75.2 1.4 multiply_add_fusion.5
  78.0 1.4 multiply_add_fusion.5
  96.9 189.4 %all_to_all.20 = bf16[8,2,32768]{2,1,0:T(2,128)(2,1)S(1)} all-to-all(bf16[8,2,32768]{2,1,0:T(2,128)(2,1)S(1)} %reshape.111), channel_id=1, replica_groups=mesh['row'=4,'col'=8] {'col'}, dimensions={0} | all-to-all | bytes 2097152 | tf_op jit(solution)/shard_map/all_to_all | solution.py:141
  288.8 2.1 copy.32
  290.9 3.6 all-to-all-start.2
  294.5 25.6 %all-to-all-done.2 = bf16[8,2,32768]{2,1,0:T(2,128)(2,1)S(1)} async-done(((bf16[8,2,32768]{2,1,0:T(2,128)(2,1)}), bf16[8,2,32768]{2,1,0:T(2,128)(2,1)S(1)}, u32[]{:S(2)}, u32[]{:S(2)}) %all-to-all-start.2) | async-done | bytes 1048608 | tf_op jit(solution)/shard_map/all_to_all | solution.py:134
  320.1 1.6 reshape.114
  322.0 55.1 %while.93 = (s32[]{:T(128)}, f32[16,32,1024]{2,1,0:T(8,128)S(1)}, f32[]{:T(128)}, s32[]{:T(128)}, s32[4,2]{0,1:T(2,128)S(1)}, /*index=5*/s32[32]{0:T(128)S(1)}, ...) while((s32[]{:T(128)}, f32[16,32,1024]{2,1,0:T(8,128)S(1)}, ...), condition=%wide.region_11.12_spmd.clone, body=%wide.region_7.11_spmd.sunk.clone.sunk | while | flops 761891 | bytes 5591080 | solution.py:90
  340.0 35.1 %while.95 = (s32[]{:T(128)}, f32[32,1024]{1,0:T(8,128)S(1)}, f32[32,1024]{1,0:T(8,128)S(1)}, f32[32,1024]{1,0:T(8,128)S(1)}, s32[]{:T(128)}, /*index=5*/f32[12]{0:T(128)S(1)}, f32[12]{0:T(128)S(1)}, s32[]{:T(128)}) while((s32[]{:T(128)}, f32[32,1024]{1,0:T(8,128)S(1)}, f32[32,1024]{1,0:T(8,128)S(1)}, ...), condition=%wide.region_9.9_spmd.clone.clone, body=%wide.region_8.8_spmd.sunk.clone.clone.sunk | while | flops 499715 | bytes 3100039 | solution.py:56
  377.2 1.6 reshape.115
  378.8 164.4 %all-to-all-start.3 = ((bf16[8,2,32768]{2,1,0:T(2,128)(2,1)}), bf16[8,2,32768]{2,1,0:T(2,128)(2,1)S(1)}, u32[]{:S(2)}, u32[]{:S(2)}) async-start(bf16[8,2,32768]{2,1,0:T(2,128)(2,1)} %reshape.115), calls=%async_computation.3 | async-start | bytes 2097152 | tf_op jit(solution)/shard_map/all_to_all | solution.py:141
  543.3 52.2 %psum.7 = f32[2]{0:T(128)S(1)} all-reduce(f32[2]{0:T(128)S(1)} %pad_maximum_fusion), channel_id=1, replica_groups=mesh['row'=4,'col'=8] {'row','col'}, use_global_device_ids=true, to_apply=%region_12.13 | all-reduce | flops 2 | bytes 16 | tf_op jit(solution)/shard_map/psum | solution.py:147
  596.8 1.5 fusion.17
  (246 shorter events, 79.0 us)
Async XLA Ops:
  0.6 14.1 %copy-start = (s32[128,3]{0,1:T(4,128)S(1)}, s32[128,3]{0,1:T(4,128)}, u32[]{:S(2)}) copy-start(s32[128,3]{0,1:T(4,128)} %param.17) | copy-start | bytes 4612
  4.1 9.4 %copy-start.7 = (s32[8]{0:T(128)S(1)}, s32[8]{0:T(128)}, u32[]{:S(2)}) copy-start(s32[8]{0:T(128)} %param.19) | copy-start | bytes 100
  6.1 33.1 %all-to-all-start = ((bf16[8,2,32768]{2,1,0:T(2,128)(2,1)}), bf16[8,2,32768]{2,1,0:T(2,128)(2,1)S(1)}, u32[]{:S(2)}, u32[]{:S(2)}) async-start(bf16[8,2,32768]{2,1,0:T(2,128)(2,1)} %copy.30), calls=%async_computation | async-start | bytes 2097152 | tf_op jit(solution)/shard_map/all_to_all | solution.py:134
  14.8 26.2 %copy-start.8 = (f32[12]{0:T(128)S(1)}, f32[12]{0:T(128)}, u32[]{:S(2)}) copy-start(f32[12]{0:T(128)} %constant.362.clone..sunk2.5) | copy-start | bytes 148
  14.8 26.3 %copy-start.9 = (f32[12]{0:T(128)S(1)}, f32[12]{0:T(128)}, u32[]{:S(2)}) copy-start(f32[12]{0:T(128)} %constant.363.clone..sunk2.5) | copy-start | bytes 148
  96.8 190.9 %copy-start.1 = (f32[4,32,1024]{2,1,0:T(8,128)S(1)}, f32[4,32,1024]{2,1,0:T(8,128)}, u32[]{:S(2)}) copy-start(f32[4,32,1024]{2,1,0:T(8,128)} %param.15) | copy-start | bytes 1572868
  96.9 190.9 %copy-start.5 = (f32[4,32,1024]{2,1,0:T(8,128)S(1)}, f32[4,32,1024]{2,1,0:T(8,128)}, u32[]{:S(2)}) copy-start(f32[4,32,1024]{2,1,0:T(8,128)} %param.16) | copy-start | bytes 1572868
  287.0 0.8 copy-start.3
  290.9 29.2 %all-to-all-start.2 = ((bf16[8,2,32768]{2,1,0:T(2,128)(2,1)}), bf16[8,2,32768]{2,1,0:T(2,128)(2,1)S(1)}, u32[]{:S(2)}, u32[]{:S(2)}) async-start(bf16[8,2,32768]{2,1,0:T(2,128)(2,1)} %copy.32), calls=%async_computation.2 | async-start | bytes 2097152 | tf_op jit(solution)/shard_map/all_to_all | solution.py:134
  378.8 218.0 %copy-start.2 = (f32[4,32,1024]{2,1,0:T(8,128)S(1)}, f32[4,32,1024]{2,1,0:T(8,128)}, u32[]{:S(2)}) copy-start(f32[4,32,1024]{2,1,0:T(8,128)} %param.15) | copy-start | bytes 1572868
  378.8 218.0 %copy-start.4 = (f32[4,32768,1]{1,0,2:T(4,128)S(1)}, f32[4,32768,1]{1,0,2:T(4,128)}, u32[]{:S(2)}) copy-start(f32[4,32768,1]{1,0,2:T(4,128)} %copy-done.3) | copy-start | bytes 1572868
  378.8 218.0 %copy-start.6 = (f32[4,32,1024]{2,1,0:T(8,128)S(1)}, f32[4,32,1024]{2,1,0:T(8,128)}, u32[]{:S(2)}) copy-start(f32[4,32,1024]{2,1,0:T(8,128)} %param.16) | copy-start | bytes 1572868
  378.8 217.3 %all-to-all-start.3 = ((bf16[8,2,32768]{2,1,0:T(2,128)(2,1)}), bf16[8,2,32768]{2,1,0:T(2,128)(2,1)S(1)}, u32[]{:S(2)}, u32[]{:S(2)}) async-start(bf16[8,2,32768]{2,1,0:T(2,128)(2,1)} %reshape.115), calls=%async_computation.3 | async-start | bytes 2097152 | tf_op jit(solution)/shard_map/all_to_all | solution.py:141
where the time goes:
time: 603 us; the launch traced here: 598 us
  blocking collectives  242 us (40%)
  starting transfers between devices  175 us (29%)
  local copies, waits for them, and re-layouts  53.3 us (9%)
  waiting for transfers between devices  50 us (8%)
  other arithmetic  43.7 us (7%)
  loops' own time  31 us (5%)
    all_to_all x1, blocking collectives, local(): lax.all_to_all(slot_terms, 'col', split_axis=0, concat_axis=0, tiled=True)  189 us
    all_to_all x1, starting transfers between devices, local(): lax.all_to_all(slot_terms, 'col', split_axis=0, concat_axis=0, tiled=True)  164 us
    psum x1, blocking collectives, local(): summed = lax.psum(jnp.stack(totals), ('row', 'col'))  52.2 us
    all_to_all x2, waiting for transfers between devices, local(): lax.all_to_all(outgoing, 'col', split_axis=0, concat_axis=0, tiled=True)  50 us
    add x24, other arithmetic, sweep(): direction = keep_coef[index] * direction + mix_coef[index] * remainder  34.3 us
    another operation x2, loops' own time, run_pairs(): lax.fori_loop(0, mine_count, one_pair, (collected, jnp.zeros((), jnp.floa...  29.8 us
    dynamic_slice x48, local copies, waits for them, and re-layouts, sweep(): direction = keep_coef[index] * direction + mix_coef[index] * remainder  29.4 us
  transfers between devices with their start and end apart: 3, of which 2 were waited for; matrix products, arithmetic and copies ran while one was open for 0% of the time, Pallas kernels for 0%

commit v1 on v0

--- a/solution.py
+++ b/solution.py
@@ -9,6 +9,28 @@
 ROUNDS = 2
 screen_mu = 0.1
 damping = 0.5
+
+
+def in_blocks(shard, dim, size):
+    before, after = (shard.shape[:dim], shard.shape[dim + 1 :])
+    return jnp.moveaxis(shard.reshape(*before, size, -1, *after), dim, 0)
+
+
+def joined_along(parts, dim):
+    shape = list(parts.shape[1:])
+    shape[dim] *= parts.shape[0]
+    return jnp.moveaxis(parts, 0, dim).reshape(shape)
+
+
+def rotated_exchange(x, axis, split_dim, concat_dim):
+    size, index = (lax.axis_size(axis), lax.axis_index(axis))
+    pieces = in_blocks(x, split_dim, size)
+    outs = [pieces[index]]
+    for step in range(1, size):
+        sent = pieces[(index + step) % size]
+        outs.append(lax.ppermute(sent, axis, [(i, (i + step) % size) for i in range(size)]))
+    pieces = jnp.stack(outs)[(index - jnp.arange(size)) % size]
+    return joined_along(pieces, concat_dim)
 
 
 def sweep_table(sweeps):
@@ -131,9 +153,7 @@
             boxes_own.reshape(own_count, edge * plane),
             preferred_element_type=jnp.float32,
         ).astype(jnp.bfloat16)
-        arrived = lax.all_to_all(outgoing, "col", split_axis=0, concat_axis=0, tiled=True).reshape(
-            slots, edge, plane
-        )
+        arrived = rotated_exchange(outgoing, "col", 0, 0).reshape(slots, edge, plane)
         gathered, energy = run_pairs(
             arrived, slot_of, slot_of, mine, mine_count, group_offsets, tables, slots
         )

time: 603 us -> 670 us (1.11)
  starting transfers between devices: 175 us -> 384 us
  blocking collectives: 242 us -> 46.2 us
  waiting for transfers between devices: 50 us -> 85.7 us
  local copies, waits for them, and re-layouts: 53.3 us -> 69 us
    all_to_all x1 -> x0, blocking collectives: 189 us -> none  [local(): lax.all_to_all(slot_terms, 'col', split_axis=0, concat_axis=0, tiled=True)]
    all_to_all x1 -> x2, starting transfers between devices: 164 us -> 350 us  [local(): lax.all_to_all(slot_terms, 'col', split_axis=0, concat_axis=0, tiled=True)]
    ppermute x0 -> x14, waiting for transfers between devices: none -> 60.5 us  [rotated_exchange(): lax.ppermute(sent, axis, [(i, (i + step) % size) for i in range(size)])]
    all_to_all x2 -> x0, waiting for transfers between devices: 50 us -> none  [local(): lax.all_to_all(outgoing, 'col', split_axis=0, concat_axis=0, tiled=True)]
    ppermute x0 -> x14, starting transfers between devices: none -> 33.7 us  [rotated_exchange(): lax.ppermute(sent, axis, [(i, (i + step) % size) for i in range(size)])]
    all_to_all x1 -> x2, waiting for transfers between devices: 0.01 us -> 25.2 us  [local(): lax.all_to_all(slot_terms, 'col', split_axis=0, concat_axis=0, tiled=True)]
    all_to_all x2 -> x0, starting transfers between devices: 10.9 us -> none  [local(): lax.all_to_all(outgoing, 'col', split_axis=0, concat_axis=0, tiled=True)]
    unnamed x20 -> x40, local copies, waits for them, and re-layouts: 0.84 us -> 8.17 us
  transfers between devices with their start and end apart: 3 -> 16, of which waited for: 2 -> 7; matrix products, arithmetic and copies ran while one was open for 0% -> 1% of each run, Pallas kernels for 0% -> 0%
where the time goes in v1:
time: 670 us; the launch traced here: 665 us
  starting transfers between devices  384 us (57%)
  waiting for transfers between devices  85.7 us (13%)
  local copies, waits for them, and re-layouts  69 us (10%)
  blocking collectives  46.2 us (7%)
  other arithmetic  44.6 us (7%)
  loops' own time  32.2 us (5%)
    all_to_all x2, starting transfers between devices, local(): lax.all_to_all(slot_terms, 'col', split_axis=0, concat_axis=0, tiled=True)  350 us
    ppermute x14, waiting for transfers between devices, rotated_exchange(): lax.ppermute(sent, axis, [(i, (i + step) % size) for i in range(size)])  60.5 us
    psum x1, blocking collectives, local(): summed = lax.psum(jnp.stack(totals), ('row', 'col'))  46.2 us
    add x24, other arithmetic, sweep(): direction = keep_coef[index] * direction + mix_coef[index] * remainder  35.1 us
    ppermute x14, starting transfers between devices, rotated_exchange(): lax.ppermute(sent, axis, [(i, (i + step) % size) for i in range(size)])  33.7 us
    another operation x2, loops' own time, run_pairs(): lax.fori_loop(0, mine_count, one_pair, (collected, jnp.zeros((), jnp.floa...  31 us
    dynamic_slice x48, local copies, waits for them, and re-layouts, sweep(): direction = keep_coef[index] * direction + mix_coef[index] * remainder  29.9 us
    all_to_all x2, waiting for transfers between devices, local(): lax.all_to_all(slot_terms, 'col', split_axis=0, concat_axis=0, tiled=True)  25.2 us
  transfers between devices with their start and end apart: 16, of which 7 were waited for; matrix products, arithmetic and copies ran while one was open for 1% of the time, Pallas kernels for 0%

profile of v1, /device:TPU:0, one launch (start us, length us, event | category | flops | bytes accessed | tf_op | source)
XLA Modules:
  0.0 664.9 jit_solution(10094902101441193077)
XLA Ops:
  4.8 2.6 constant_dynamic-slice_fusion.17
  7.4 6.1 collective-permute-start.6
  13.9 3.0 collective-permute-start.3
  20.1 17.1 %collective-permute-done = bf16[1,2,32768]{2,0,1:T(2,128)(2,1)} collective-permute-done((bf16[1,2,32768]{2,0,1:T(2,128)(2,1)S(1)}, bf16[1,2,32768]{2,0,1:T(2,128)(2,1)}, u32[]{:S(2)}, u32[]{:S(2)}) %collective-permute-start) | collective-permute-done | bytes 131104 | tf_op jit(solution)/shard_map/ppermute | solution.py:31
  40.1 5.9 collective-permute-done.1
  46.0 5.5 collective-permute-start.2
  51.7 5.4 collective-permute-done.2
  61.1 2.7 gather_fusion
  65.7 55.5 %while.91 = (s32[]{:T(128)}, f32[16,32,1024]{2,1,0:T(8,128)S(1)}, f32[]{:T(128)}, s32[]{:T(128)}, s32[4,2]{0,1:T(2,128)S(1)}, /*index=5*/s32[32]{0:T(128)S(1)}, ...) while((s32[]{:T(128)}, f32[16,32,1024]{2,1,0:T(8,128)S(1)}, ...), condition=%wide.region_6.7_spmd.clone, body=%wide.region_2.6_spmd.sunk.clone.sunk | while | flops 761891 | bytes 5591096 | solution.py:112
  84.1 35.0 %while.94 = (s32[]{:T(128)}, f32[32,1024]{1,0:T(8,128)S(1)}, f32[32,1024]{1,0:T(8,128)S(1)}, f32[32,1024]{1,0:T(8,128)S(1)}, s32[]{:T(128)}, /*index=5*/f32[12]{0:T(128)S(1)}, f32[12]{0:T(128)S(1)}, s32[]{:T(128)}) while((s32[]{:T(128)}, f32[32,1024]{1,0:T(8,128)S(1)}, f32[32,1024]{1,0:T(8,128)S(1)}, ...), condition=%wide.region_4.4_spmd.clone.clone, body=%wide.region_3.3_spmd.sunk.clone.clone.sunk | while | flops 499715 | bytes 3100039 | solution.py:78
  122.9 173.0 %all-to-all-start = ((bf16[8,2,32768]{2,1,0:T(2,128)(2,1)}), bf16[8,2,32768]{2,1,0:T(2,128)(2,1)S(1)}, u32[]{:S(2)}, u32[]{:S(2)}) async-start(bf16[8,2,32768]{2,1,0:T(2,128)(2,1)} %reshape.185), calls=%async_computation | async-start | bytes 2097152 | tf_op jit(solution)/shard_map/all_to_all | solution.py:161
  295.9 25.2 %all-to-all-done = bf16[8,2,32768]{2,1,0:T(2,128)(2,1)S(1)} async-done(((bf16[8,2,32768]{2,1,0:T(2,128)(2,1)}), bf16[8,2,32768]{2,1,0:T(2,128)(2,1)S(1)}, u32[]{:S(2)}, u32[]{:S(2)}) %all-to-all-start) | async-done | bytes 1048608 | tf_op jit(solution)/shard_map/all_to_all | solution.py:161
  323.7 2.6 constant_dynamic-slice_fusion.8
  326.3 2.9 collective-permute-start.13
  329.2 3.3 collective-permute-start.10
  334.4 18.6 %collective-permute-done.7 = bf16[1,2,32768]{2,0,1:T(2,128)(2,1)S(1)} collective-permute-done((bf16[1,2,32768]{2,0,1:T(2,128)(2,1)S(1)}, bf16[1,2,32768]{2,0,1:T(2,128)(2,1)S(1)}, u32[]{:S(2)}, u32[]{:S(2)}) %collective-permute-start.7) | collective-permute-done | bytes 131104 | tf_op jit(solution)/shard_map/ppermute | solution.py:31
  355.8 7.8 %collective-permute-done.8 = bf16[1,2,32768]{2,0,1:T(2,128)(2,1)S(1)} collective-permute-done((bf16[1,2,32768]{2,0,1:T(2,128)(2,1)S(1)}, bf16[1,2,32768]{2,0,1:T(2,128)(2,1)S(1)}, u32[]{:S(2)}, u32[]{:S(2)}) %collective-permute-start.8) | collective-permute-done | bytes 131104 | tf_op jit(solution)/shard_map/ppermute | solution.py:31
  363.6 5.0 collective-permute-start.9
  368.8 5.6 collective-permute-done.9
  375.6 2.8 gather_fusion.1
  380.2 56.9 %while.93 = (s32[]{:T(128)}, f32[16,32,1024]{2,1,0:T(8,128)S(1)}, f32[]{:T(128)}, s32[]{:T(128)}, s32[4,2]{0,1:T(2,128)S(1)}, /*index=5*/s32[32]{0:T(128)S(1)}, ...) while((s32[]{:T(128)}, f32[16,32,1024]{2,1,0:T(8,128)S(1)}, ...), condition=%wide.region_11.12_spmd.clone, body=%wide.region_7.11_spmd.sunk.clone.sunk | while | flops 761891 | bytes 5591080 | solution.py:112
  399.0 36.1 %while.95 = (s32[]{:T(128)}, f32[32,1024]{1,0:T(8,128)S(1)}, f32[32,1024]{1,0:T(8,128)S(1)}, f32[32,1024]{1,0:T(8,128)S(1)}, s32[]{:T(128)}, /*index=5*/f32[12]{0:T(128)S(1)}, f32[12]{0:T(128)S(1)}, s32[]{:T(128)}) while((s32[]{:T(128)}, f32[32,1024]{1,0:T(8,128)S(1)}, f32[32,1024]{1,0:T(8,128)S(1)}, ...), condition=%wide.region_9.9_spmd.clone.clone, body=%wide.region_8.8_spmd.sunk.clone.clone.sunk | while | flops 499715 | bytes 3100039 | solution.py:78
  438.9 177.0 %all-to-all-start.1 = ((bf16[8,2,32768]{2,1,0:T(2,128)(2,1)}), bf16[8,2,32768]{2,1,0:T(2,128)(2,1)S(1)}, u32[]{:S(2)}, u32[]{:S(2)}) async-start(bf16[8,2,32768]{2,1,0:T(2,128)(2,1)} %reshape.188), calls=%async_computation.1 | async-start | bytes 2097152 | tf_op jit(solution)/shard_map/all_to_all | solution.py:161
  616.0 46.2 %psum.7 = f32[2]{0:T(128)S(1)} all-reduce(f32[2]{0:T(128)S(1)} %pad_maximum_fusion), channel_id=1, replica_groups=mesh['row'=4,'col'=8] {'row','col'}, use_global_device_ids=true, to_apply=%region_12.13 | all-reduce | flops 2 | bytes 16 | tf_op jit(solution)/shard_map/psum | solution.py:167
  (297 shorter events, 113.3 us)
Async XLA Ops:
  0.6 18.1 %copy-start = (s32[128,3]{0,1:T(4,128)S(1)}, s32[128,3]{0,1:T(4,128)}, u32[]{:S(2)}) copy-start(s32[128,3]{0,1:T(4,128)} %param.17) | copy-start | bytes 4612
  7.4 53.5 %collective-permute-start.6 = (bf16[1,2,32768]{2,0,1:T(2,128)(2,1)S(1)}, bf16[1,2,32768]{2,0,1:T(2,128)(2,1)S(1)}, u32[]{:S(2)}, u32[]{:S(2)}) collective-permute-start(bf16[1,2,32768]{2,0,1:T(2,128)(2,1)S(1)} %get-tuple-element.840), channel_id=1, source_target_pairs={{0,7},{1,0},{2,1},{3,2},{4,3},{5,4},{6,5},{7,6},{8,15},{9,8},{10,9... | collective-permute-start | bytes 393224 | tf_op jit(solution)/shard_map/ppermute | solution.py:31
  13.5 46.2 %collective-permute-start.5 = (bf16[1,2,32768]{2,0,1:T(2,128)(2,1)S(1)}, bf16[1,2,32768]{2,0,1:T(2,128)(2,1)}, u32[]{:S(2)}, u32[]{:S(2)}) collective-permute-start(bf16[1,2,32768]{2,0,1:T(2,128)(2,1)S(1)} %get-tuple-element.841), channel_id=1, source_target_pairs={{0,6},{1,7},{2,0},{3,1},{4,2},{5,3},{6,4},{7,5},{8,14},{9,15},{10,... | collective-permute-start | bytes 393224 | tf_op jit(solution)/shard_map/ppermute | solution.py:31
  13.9 44.6 %collective-permute-start.4 = (bf16[1,2,32768]{2,0,1:T(2,128)(2,1)S(1)}, bf16[1,2,32768]{2,0,1:T(2,128)(2,1)}, u32[]{:S(2)}, u32[]{:S(2)}) collective-permute-start(bf16[1,2,32768]{2,0,1:T(2,128)(2,1)S(1)} %get-tuple-element.842), channel_id=1, source_target_pairs={{0,5},{1,6},{2,7},{3,0},{4,1},{5,2},{6,3},{7,4},{8,13},{9,14},{10,... | collective-permute-start | bytes 393224 | tf_op jit(solution)/shard_map/ppermute | solution.py:31
  13.9 43.4 %collective-permute-start.3 = (bf16[1,2,32768]{2,0,1:T(2,128)(2,1)S(1)}, bf16[1,2,32768]{2,0,1:T(2,128)(2,1)}, u32[]{:S(2)}, u32[]{:S(2)}) collective-permute-start(bf16[1,2,32768]{2,0,1:T(2,128)(2,1)S(1)} %get-tuple-element.843), channel_id=1, source_target_pairs={{0,4},{1,5},{2,6},{3,7},{4,0},{5,1},{6,2},{7,3},{8,12},{9,13},{10,... | collective-permute-start | bytes 393224 | tf_op jit(solution)/shard_map/ppermute | solution.py:31
  16.9 20.3 %collective-permute-start = (bf16[1,2,32768]{2,0,1:T(2,128)(2,1)S(1)}, bf16[1,2,32768]{2,0,1:T(2,128)(2,1)}, u32[]{:S(2)}, u32[]{:S(2)}) collective-permute-start(bf16[1,2,32768]{2,0,1:T(2,128)(2,1)S(1)} %get-tuple-element.846), channel_id=1, source_target_pairs={{0,1},{1,2},{2,3},{3,4},{4,5},{5,6},{6,7},{7,0},{8,9},{9,10},{10,1... | collective-permute-start | bytes 393224 | tf_op jit(solution)/shard_map/ppermute | solution.py:31
  20.1 43.7 %copy-start.9 = (s32[1024]{0:T(1024)}, s32[1024]{0:T(1024)S(1)}, u32[]{:S(2)}) copy-start(s32[1024]{0:T(1024)S(1)} %pad_clamp_fusion) | copy-start | bytes 12292
  37.2 8.8 %collective-permute-start.1 = (bf16[1,2,32768]{2,0,1:T(2,128)(2,1)S(1)}, bf16[1,2,32768]{2,0,1:T(2,128)(2,1)S(1)}, u32[]{:S(2)}, u32[]{:S(2)}) collective-permute-start(bf16[1,2,32768]{2,0,1:T(2,128)(2,1)S(1)} %get-tuple-element.845), channel_id=1, source_target_pairs={{0,2},{1,3},{2,4},{3,5},{4,6},{5,7},{6,0},{7,1},{8,10},{9,11},{10,... | collective-permute-start | bytes 393224 | tf_op jit(solution)/shard_map/ppermute | solution.py:31
  46.0 11.2 %collective-permute-start.2 = (bf16[1,2,32768]{2,0,1:T(2,128)(2,1)S(1)}, bf16[1,2,32768]{2,0,1:T(2,128)(2,1)S(1)}, u32[]{:S(2)}, u32[]{:S(2)}) collective-permute-start(bf16[1,2,32768]{2,0,1:T(2,128)(2,1)S(1)} %get-tuple-element.844), channel_id=1, source_target_pairs={{0,3},{1,4},{2,5},{3,6},{4,7},{5,0},{6,1},{7,2},{8,11},{9,12},{10,... | collective-permute-start | bytes 393224 | tf_op jit(solution)/shard_map/ppermute | solution.py:31
  121.3 199.7 %copy-start.8 = (pred[8,2,4]{0,2,1:T(4,128)(4,1)S(1)}, pred[8,2,4]{0,2,1:T(4,128)(4,1)}, u32[]{:S(2)}) copy-start(pred[8,2,4]{0,2,1:T(4,128)(4,1)} %copy-done.7) | copy-start | bytes 196
  122.9 199.7 %copy-start.1 = (f32[4,32,1024]{2,1,0:T(8,128)S(1)}, f32[4,32,1024]{2,1,0:T(8,128)}, u32[]{:S(2)}) copy-start(f32[4,32,1024]{2,1,0:T(8,128)} %param.15) | copy-start | bytes 1572868
  122.9 199.7 %copy-start.5 = (f32[4,32,1024]{2,1,0:T(8,128)S(1)}, f32[4,32,1024]{2,1,0:T(8,128)}, u32[]{:S(2)}) copy-start(f32[4,32,1024]{2,1,0:T(8,128)} %param.16) | copy-start | bytes 1572868
  122.9 198.1 %all-to-all-start = ((bf16[8,2,32768]{2,1,0:T(2,128)(2,1)}), bf16[8,2,32768]{2,1,0:T(2,128)(2,1)S(1)}, u32[]{:S(2)}, u32[]{:S(2)}) async-start(bf16[8,2,32768]{2,1,0:T(2,128)(2,1)} %reshape.185), calls=%async_computation | async-start | bytes 2097152 | tf_op jit(solution)/shard_map/all_to_all | solution.py:161
  326.3 49.0 %collective-permute-start.13 = (bf16[1,2,32768]{2,0,1:T(2,128)(2,1)S(1)}, bf16[1,2,32768]{2,0,1:T(2,128)(2,1)S(1)}, u32[]{:S(2)}, u32[]{:S(2)}) collective-permute-start(bf16[1,2,32768]{2,0,1:T(2,128)(2,1)S(1)} %get-tuple-element.832), channel_id=1, source_target_pairs={{0,7},{1,0},{2,1},{3,2},{4,3},{5,4},{6,5},{7,6},{8,15},{9,8},{10,9... | collective-permute-start | bytes 393224 | tf_op jit(solution)/shard_map/ppermute | solution.py:31
  329.2 45.9 %collective-permute-start.12 = (bf16[1,2,32768]{2,0,1:T(2,128)(2,1)S(1)}, bf16[1,2,32768]{2,0,1:T(2,128)(2,1)S(1)}, u32[]{:S(2)}, u32[]{:S(2)}) collective-permute-start(bf16[1,2,32768]{2,0,1:T(2,128)(2,1)S(1)} %get-tuple-element.833), channel_id=1, source_target_pairs={{0,6},{1,7},{2,0},{3,1},{4,2},{5,3},{6,4},{7,5},{8,14},{9,15},{10,... | collective-permute-start | bytes 393224 | tf_op jit(solution)/shard_map/ppermute | solution.py:31
  329.2 45.7 %collective-permute-start.11 = (bf16[1,2,32768]{2,0,1:T(2,128)(2,1)S(1)}, bf16[1,2,32768]{2,0,1:T(2,128)(2,1)S(1)}, u32[]{:S(2)}, u32[]{:S(2)}) collective-permute-start(bf16[1,2,32768]{2,0,1:T(2,128)(2,1)S(1)} %get-tuple-element.834), channel_id=1, source_target_pairs={{0,5},{1,6},{2,7},{3,0},{4,1},{5,2},{6,3},{7,4},{8,13},{9,14},{10,... | collective-permute-start | bytes 393224 | tf_op jit(solution)/shard_map/ppermute | solution.py:31
  329.2 45.4 %collective-permute-start.10 = (bf16[1,2,32768]{2,0,1:T(2,128)(2,1)S(1)}, bf16[1,2,32768]{2,0,1:T(2,128)(2,1)S(1)}, u32[]{:S(2)}, u32[]{:S(2)}) collective-permute-start(bf16[1,2,32768]{2,0,1:T(2,128)(2,1)S(1)} %get-tuple-element.835), channel_id=1, source_target_pairs={{0,4},{1,5},{2,6},{3,7},{4,0},{5,1},{6,2},{7,3},{8,12},{9,13},{10,... | collective-permute-start | bytes 393224 | tf_op jit(solution)/shard_map/ppermute | solution.py:31
  332.5 20.5 %collective-permute-start.7 = (bf16[1,2,32768]{2,0,1:T(2,128)(2,1)S(1)}, bf16[1,2,32768]{2,0,1:T(2,128)(2,1)S(1)}, u32[]{:S(2)}, u32[]{:S(2)}) collective-permute-start(bf16[1,2,32768]{2,0,1:T(2,128)(2,1)S(1)} %get-tuple-element.838), channel_id=1, source_target_pairs={{0,1},{1,2},{2,3},{3,4},{4,5},{5,6},{6,7},{7,0},{8,9},{9,10},{10,1... | collective-permute-start | bytes 393224 | tf_op jit(solution)/shard_map/ppermute | solution.py:31
  353.0 10.6 %collective-permute-start.8 = (bf16[1,2,32768]{2,0,1:T(2,128)(2,1)S(1)}, bf16[1,2,32768]{2,0,1:T(2,128)(2,1)S(1)}, u32[]{:S(2)}, u32[]{:S(2)}) collective-permute-start(bf16[1,2,32768]{2,0,1:T(2,128)(2,1)S(1)} %get-tuple-element.837), channel_id=1, source_target_pairs={{0,2},{1,3},{2,4},{3,5},{4,6},{5,7},{6,0},{7,1},{8,10},{9,11},{10,... | collective-permute-start | bytes 393224 | tf_op jit(solution)/shard_map/ppermute | solution.py:31
  363.6 10.8 %collective-permute-start.9 = (bf16[1,2,32768]{2,0,1:T(2,128)(2,1)S(1)}, bf16[1,2,32768]{2,0,1:T(2,128)(2,1)S(1)}, u32[]{:S(2)}, u32[]{:S(2)}) collective-permute-start(bf16[1,2,32768]{2,0,1:T(2,128)(2,1)S(1)} %get-tuple-element.836), channel_id=1, source_target_pairs={{0,3},{1,4},{2,5},{3,6},{4,7},{5,0},{6,1},{7,2},{8,11},{9,12},{10,... | collective-permute-start | bytes 393224 | tf_op jit(solution)/shard_map/ppermute | solution.py:31
  438.9 224.5 %copy-start.2 = (f32[4,32,1024]{2,1,0:T(8,128)S(1)}, f32[4,32,1024]{2,1,0:T(8,128)}, u32[]{:S(2)}) copy-start(f32[4,32,1024]{2,1,0:T(8,128)} %param.15) | copy-start | bytes 1572868
  438.9 224.5 %copy-start.4 = (f32[4,32768,1]{1,0,2:T(4,128)S(1)}, f32[4,32768,1]{1,0,2:T(4,128)}, u32[]{:S(2)}) copy-start(f32[4,32768,1]{1,0,2:T(4,128)} %copy-done.3) | copy-start | bytes 1572868
  438.9 224.5 %copy-start.6 = (f32[4,32,1024]{2,1,0:T(8,128)S(1)}, f32[4,32,1024]{2,1,0:T(8,128)}, u32[]{:S(2)}) copy-start(f32[4,32,1024]{2,1,0:T(8,128)} %param.16) | copy-start | bytes 1572868
  438.9 223.8 %all-to-all-start.1 = ((bf16[8,2,32768]{2,1,0:T(2,128)(2,1)}), bf16[8,2,32768]{2,1,0:T(2,128)(2,1)S(1)}, u32[]{:S(2)}, u32[]{:S(2)}) async-start(bf16[8,2,32768]{2,1,0:T(2,128)(2,1)} %reshape.188), calls=%async_computation.1 | async-start | bytes 2097152 | tf_op jit(solution)/shard_map/all_to_all | solution.py:161
  (5 other events, 19.2 us)
